TPU v7x, 32 devices: a whole 2x2x4 slice. The times are simulated.
32 devices in a mesh: runs: 2 (over y), ja: 16 (over z, x, core).
Axes of the slice: x: 2, y: 2, z: 4, core: 2. Of those that a mesh axis runs over, the one named last changes fastest.
Arguments:
- pos_vel: float32 [6, 32768], P(None, ('runs', 'ja')), parts along dimension 1, may hold values from -4 to 4
- acc_jerk: float32 [6, 32768], P(None, ('runs', 'ja')), parts along dimension 1, may hold values from -5 to 5
- star_mass: float32 [32768], P(('runs', 'ja')), parts along dimension 0, may hold values from 1.2207031e-05 to 0.00030517578
- step_phase: float32 [32768], P(('runs', 'ja')), parts along dimension 0, may hold values from 0.25 to 1
- step_level: int32 [32768], P(('runs', 'ja')), parts along dimension 0, may hold values from 0 to 3
- counts: int32 [32], P(('runs', 'ja')), parts along dimension 0, may hold values from 1 to 256, 2048 in all
- star_order: int32 [32, 1024], P(('runs', 'ja')), parts along dimension 0, may hold values from 0 to 1023, each once within a row
Outputs:
- new_pos_vel: float32 [6, 32768], P(None, ('runs', 'ja')), parts along dimension 1
- new_acc_jerk: float32 [6, 32768], P(None, ('runs', 'ja')), parts along dimension 1
- active_state: float32 [12, 8192], P(None, ('runs', 'ja')), parts along dimension 1
There are 2 independent parts, one for each index of `runs`. A program takes and returns all parts, laid end to end along the dimension named above; each array names one. Nothing has to cross between parts.
Inputs may be any that keep to these rules, and one draw needn't show every extreme that they name: The counts sum to 2048; the largest is exactly 256. `star_order`: each row is a permutation of the local indices.
All inputs are finite; a program needn't handle non-finite values. No bound on the sum of `counts` on one device may be relied on, other than what follows from the above.
Results may differ from a plain program's by a relative error of at most 0.00002.
Values sent between devices are 32-bit elements; how exact they have to be, the bound alone decides.
A program may use at most 64 MiB of HBM per device.

v0:
```python
import math

import jax
import jax.numpy as jnp
from jax import lax
from jax.sharding import PartitionSpec as P

A_DEV = 128


soft_sq = 0.01
base_step = 2.0


def predict(pos_vel, acc_jerk, age):
    half_sq = 0.5 * age * age
    sixth_cube = age * age * age / 6.0
    position = (
        pos_vel[0:3] + age * pos_vel[3:6] + half_sq * acc_jerk[0:3] + sixth_cube * acc_jerk[3:6]
    )
    velocity = pos_vel[3:6] + age * acc_jerk[0:3] + half_sq * acc_jerk[3:6]
    return jnp.concatenate([position, velocity], axis=0)


def pair_block(targets, sources):
    delta_x = sources[0:3, None, :] - targets[0:3, :, None]
    delta_v = sources[3:6, None, :] - targets[3:6, :, None]
    dist_sq = soft_sq + delta_x[0] * delta_x[0] + delta_x[1] * delta_x[1] + delta_x[2] * delta_x[2]
    inverse = lax.rsqrt(dist_sq)
    inverse_sq = inverse * inverse
    weight = sources[6][None, :] * inverse * inverse_sq
    radial = (
        3.0
        * (delta_x[0] * delta_v[0] + delta_x[1] * delta_v[1] + delta_x[2] * delta_v[2])
        * inverse_sq
    )
    accel_part = jnp.sum(weight[None] * delta_x, axis=2)
    jerk_part = jnp.sum(weight[None] * (delta_v - radial[None] * delta_x), axis=2)
    return jnp.concatenate([accel_part, jerk_part], axis=0)


def pair_forces(targets, sources):
    rows = targets.shape[1]
    block = math.gcd(rows, 512)
    split = targets.reshape(6, rows // block, block).transpose(1, 0, 2)
    result = lax.map(lambda part: pair_block(part, sources), split)
    return result.transpose(1, 0, 2).reshape(6, rows)


def correct(old_pv, old_aj, fresh, step_len):
    half = 0.5 * step_len
    twelfth = step_len * step_len / 12.0
    velocity = (
        old_pv[3:6] + half * (old_aj[0:3] + fresh[0:3]) + twelfth * (old_aj[3:6] - fresh[3:6])
    )
    position = old_pv[0:3] + half * (old_pv[3:6] + velocity) + twelfth * (old_aj[0:3] - fresh[0:3])
    return jnp.concatenate([position, velocity], axis=0)


def per_device(pos_vel, acc_jerk, star_mass, step_phase, step_level, counts, star_order):
    capacity = 2 * A_DEV
    per_owner = pos_vel.shape[1]
    slot_ids = star_order[0, :capacity]
    live = jnp.arange(capacity, dtype=jnp.int32) < counts[0]
    step_len = base_step * jnp.exp2(-step_level.astype(jnp.float32))
    is_active = jnp.zeros((per_owner,), jnp.float32).at[slot_ids].set(live.astype(jnp.float32))
    age = step_len * jnp.where(is_active > 0.5, jnp.float32(1.0), step_phase)
    predicted = predict(pos_vel, acc_jerk, age)
    sources = jnp.concatenate([predicted, star_mass[None, :]], axis=0)
    targets = predicted[:, slot_ids]
    every_slot = pair_forces(lax.all_gather(targets, "ja", axis=1, tiled=True), sources)
    fresh = lax.psum_scatter(every_slot, "ja", scatter_dimension=1, tiled=True)
    old_pv = pos_vel[:, slot_ids]
    old_aj = acc_jerk[:, slot_ids]
    corrected = correct(old_pv, old_aj, fresh, step_len[slot_ids])
    kept_pv = jnp.where(live[None, :], corrected, old_pv)
    kept_aj = jnp.where(live[None, :], fresh, old_aj)
    fresh_state = jnp.concatenate([corrected, fresh], axis=0)
    active_state = jnp.where(live[None, :], fresh_state, jnp.zeros_like(fresh_state))
    return (
        pos_vel.at[:, slot_ids].set(kept_pv),
        acc_jerk.at[:, slot_ids].set(kept_aj),
        active_state,
    )


def solution(mesh):
    in_specs = (
        P(None, ("runs", "ja")),
        P(None, ("runs", "ja")),
        P(("runs", "ja")),
        P(("runs", "ja")),
        P(("runs", "ja")),
        P(("runs", "ja")),
        P(("runs", "ja"), None),
    )
    out_specs = (P(None, ("runs", "ja")), P(None, ("runs", "ja")), P(None, ("runs", "ja")))
    return jax.shard_map(
        per_device, mesh=mesh, in_specs=in_specs, out_specs=out_specs, check_vma=False
    )
```

profile of v0, /device:TPU:0, one launch (start us, length us, event | category | flops | bytes accessed | tf_op | source)
XLA Modules:
  0.0 163.4 jit_solution(9039283092665602739)
XLA Ops:
  7.2 0.7 compare_select_fusion
  8.6 1.4 scatter_custom_fusion
  10.0 0.7 multiply_multiply_fusion.1
  10.7 0.9 multiply_add_fusion
  11.6 0.2 copy.81
  11.8 0.7 gather_fusion.3
  12.6 32.3 %all-gather = f32[6,4096]{0,1:T(8,128)S(1)} all-gather(f32[6,256]{0,1:T(8,128)S(1)} %bitcast.44), channel_id=2, replica_groups=mesh['runs'=2,'ja'=16] {'ja'}, dimensions={1}, use_global_device_ids=true | all-gather | bytes 104448 | tf_op jit(solution)/shard_map/all_gather | solution.py:71
  44.8 0.6 copy.82
  45.5 45.8 %while.10 = (s32[]{:T(128)}, f32[8,6,512]{2,1,0:T(8,128)S(1)}, f32[1,1024]{1,0:T(1,128)S(1)}, f32[3,1024]{1,0:T(4,128)S(1)}, f32[8,6,512]{2,1,0:T(8,128)S(1)}, /...) while((s32[]{:T(128)}, f32[8,6,512]{2,1,0:T(8,128)S(1)}, f32[1,1024]{1,0:T(1,128)S(1)}, ...), condition=%wide.region_4.5_spmd, body=%wide.region_1.4_spmd.sunk | while | flops 24117252 | bytes 33702004 | solution.py:46
  45.5 1.1 broadcast_subtract_fusion.3
  46.6 2.1 %fusion.17 = (f32[512,1024]{1,0:T(8,128)S(1)}, f32[512,1024]{1,0:T(8,128)S(1)}) fusion(f32[3,512,1024]{2,1,0:T(8,128)S(1)} %get-tuple-element.141, f32[3,512,1024]{2,1,0:T(8,128)S(1)} %get-tuple-element.142, f32[1024]{0:T(1024)S(1)} %bitcast.47), kind=kLoop, calls=%fused_computation.15.clone.1 | loop fusion | flops 8388608 | bytes 16781312 | tf_op jit(solution)/shard_map/while/body/eval_jaxpr/mul | solution.py:38
  48.7 2.5 %multiply_reduce_fusion.3 = (f32[3,512]{1,0:T(4,128)S(1)}, f32[3,512]{1,0:T(4,128)S(1)}) fusion(f32[512,1024]{1,0:T(8,128)S(1)} %get-tuple-element.143, f32[3,512]{1,0:T(4,128)S(1)} %get-tuple-element.140, f32[3,1024]{1,0:T(4,128)S(1)} %get-tuple-element.168, f32[512,1024]{1,0:T(8,128)S(1)} %get-tuple-element.144, ...), kind=kLoop, calls=%fused_computation.8.clone.1 | loop fusion | flops 12579840 | bytes 4243456 | tf_op jit(solution)/shard_map/while/body/eval_jaxpr/reduce_sum | solution.py:37
  51.2 1.1 broadcast_subtract_fusion.3
  52.3 2.1 %fusion.17 = (f32[512,1024]{1,0:T(8,128)S(1)}, f32[512,1024]{1,0:T(8,128)S(1)}) fusion(f32[3,512,1024]{2,1,0:T(8,128)S(1)} %get-tuple-element.141, f32[3,512,1024]{2,1,0:T(8,128)S(1)} %get-tuple-element.142, f32[1024]{0:T(1024)S(1)} %bitcast.47), kind=kLoop, calls=%fused_computation.15.clone.1 | loop fusion | flops 8388608 | bytes 16781312 | tf_op jit(solution)/shard_map/while/body/eval_jaxpr/mul | solution.py:38
  54.4 2.5 %multiply_reduce_fusion.3 = (f32[3,512]{1,0:T(4,128)S(1)}, f32[3,512]{1,0:T(4,128)S(1)}) fusion(f32[512,1024]{1,0:T(8,128)S(1)} %get-tuple-element.143, f32[3,512]{1,0:T(4,128)S(1)} %get-tuple-element.140, f32[3,1024]{1,0:T(4,128)S(1)} %get-tuple-element.168, f32[512,1024]{1,0:T(8,128)S(1)} %get-tuple-element.144, ...), kind=kLoop, calls=%fused_computation.8.clone.1 | loop fusion | flops 12579840 | bytes 4243456 | tf_op jit(solution)/shard_map/while/body/eval_jaxpr/reduce_sum | solution.py:37
  56.9 1.1 broadcast_subtract_fusion.3
  58.0 2.1 %fusion.17 = (f32[512,1024]{1,0:T(8,128)S(1)}, f32[512,1024]{1,0:T(8,128)S(1)}) fusion(f32[3,512,1024]{2,1,0:T(8,128)S(1)} %get-tuple-element.141, f32[3,512,1024]{2,1,0:T(8,128)S(1)} %get-tuple-element.142, f32[1024]{0:T(1024)S(1)} %bitcast.47), kind=kLoop, calls=%fused_computation.15.clone.1 | loop fusion | flops 8388608 | bytes 16781312 | tf_op jit(solution)/shard_map/while/body/eval_jaxpr/mul | solution.py:38
  60.1 2.5 %multiply_reduce_fusion.3 = (f32[3,512]{1,0:T(4,128)S(1)}, f32[3,512]{1,0:T(4,128)S(1)}) fusion(f32[512,1024]{1,0:T(8,128)S(1)} %get-tuple-element.143, f32[3,512]{1,0:T(4,128)S(1)} %get-tuple-element.140, f32[3,1024]{1,0:T(4,128)S(1)} %get-tuple-element.168, f32[512,1024]{1,0:T(8,128)S(1)} %get-tuple-element.144, ...), kind=kLoop, calls=%fused_computation.8.clone.1 | loop fusion | flops 12579840 | bytes 4243456 | tf_op jit(solution)/shard_map/while/body/eval_jaxpr/reduce_sum | solution.py:37
  62.7 1.1 broadcast_subtract_fusion.3
  63.7 2.1 %fusion.17 = (f32[512,1024]{1,0:T(8,128)S(1)}, f32[512,1024]{1,0:T(8,128)S(1)}) fusion(f32[3,512,1024]{2,1,0:T(8,128)S(1)} %get-tuple-element.141, f32[3,512,1024]{2,1,0:T(8,128)S(1)} %get-tuple-element.142, f32[1024]{0:T(1024)S(1)} %bitcast.47), kind=kLoop, calls=%fused_computation.15.clone.1 | loop fusion | flops 8388608 | bytes 16781312 | tf_op jit(solution)/shard_map/while/body/eval_jaxpr/mul | solution.py:38
  65.8 2.5 %multiply_reduce_fusion.3 = (f32[3,512]{1,0:T(4,128)S(1)}, f32[3,512]{1,0:T(4,128)S(1)}) fusion(f32[512,1024]{1,0:T(8,128)S(1)} %get-tuple-element.143, f32[3,512]{1,0:T(4,128)S(1)} %get-tuple-element.140, f32[3,1024]{1,0:T(4,128)S(1)} %get-tuple-element.168, f32[512,1024]{1,0:T(8,128)S(1)} %get-tuple-element.144, ...), kind=kLoop, calls=%fused_computation.8.clone.1 | loop fusion | flops 12579840 | bytes 4243456 | tf_op jit(solution)/shard_map/while/body/eval_jaxpr/reduce_sum | solution.py:37
  68.4 1.1 broadcast_subtract_fusion.3
  69.5 2.1 %fusion.17 = (f32[512,1024]{1,0:T(8,128)S(1)}, f32[512,1024]{1,0:T(8,128)S(1)}) fusion(f32[3,512,1024]{2,1,0:T(8,128)S(1)} %get-tuple-element.141, f32[3,512,1024]{2,1,0:T(8,128)S(1)} %get-tuple-element.142, f32[1024]{0:T(1024)S(1)} %bitcast.47), kind=kLoop, calls=%fused_computation.15.clone.1 | loop fusion | flops 8388608 | bytes 16781312 | tf_op jit(solution)/shard_map/while/body/eval_jaxpr/mul | solution.py:38
  71.5 2.5 %multiply_reduce_fusion.3 = (f32[3,512]{1,0:T(4,128)S(1)}, f32[3,512]{1,0:T(4,128)S(1)}) fusion(f32[512,1024]{1,0:T(8,128)S(1)} %get-tuple-element.143, f32[3,512]{1,0:T(4,128)S(1)} %get-tuple-element.140, f32[3,1024]{1,0:T(4,128)S(1)} %get-tuple-element.168, f32[512,1024]{1,0:T(8,128)S(1)} %get-tuple-element.144, ...), kind=kLoop, calls=%fused_computation.8.clone.1 | loop fusion | flops 12579840 | bytes 4243456 | tf_op jit(solution)/shard_map/while/body/eval_jaxpr/reduce_sum | solution.py:37
  74.1 1.1 broadcast_subtract_fusion.3
  75.2 2.1 %fusion.17 = (f32[512,1024]{1,0:T(8,128)S(1)}, f32[512,1024]{1,0:T(8,128)S(1)}) fusion(f32[3,512,1024]{2,1,0:T(8,128)S(1)} %get-tuple-element.141, f32[3,512,1024]{2,1,0:T(8,128)S(1)} %get-tuple-element.142, f32[1024]{0:T(1024)S(1)} %bitcast.47), kind=kLoop, calls=%fused_computation.15.clone.1 | loop fusion | flops 8388608 | bytes 16781312 | tf_op jit(solution)/shard_map/while/body/eval_jaxpr/mul | solution.py:38
  77.3 2.5 %multiply_reduce_fusion.3 = (f32[3,512]{1,0:T(4,128)S(1)}, f32[3,512]{1,0:T(4,128)S(1)}) fusion(f32[512,1024]{1,0:T(8,128)S(1)} %get-tuple-element.143, f32[3,512]{1,0:T(4,128)S(1)} %get-tuple-element.140, f32[3,1024]{1,0:T(4,128)S(1)} %get-tuple-element.168, f32[512,1024]{1,0:T(8,128)S(1)} %get-tuple-element.144, ...), kind=kLoop, calls=%fused_computation.8.clone.1 | loop fusion | flops 12579840 | bytes 4243456 | tf_op jit(solution)/shard_map/while/body/eval_jaxpr/reduce_sum | solution.py:37
  79.8 1.1 broadcast_subtract_fusion.3
  80.9 2.1 %fusion.17 = (f32[512,1024]{1,0:T(8,128)S(1)}, f32[512,1024]{1,0:T(8,128)S(1)}) fusion(f32[3,512,1024]{2,1,0:T(8,128)S(1)} %get-tuple-element.141, f32[3,512,1024]{2,1,0:T(8,128)S(1)} %get-tuple-element.142, f32[1024]{0:T(1024)S(1)} %bitcast.47), kind=kLoop, calls=%fused_computation.15.clone.1 | loop fusion | flops 8388608 | bytes 16781312 | tf_op jit(solution)/shard_map/while/body/eval_jaxpr/mul | solution.py:38
  83.0 2.5 %multiply_reduce_fusion.3 = (f32[3,512]{1,0:T(4,128)S(1)}, f32[3,512]{1,0:T(4,128)S(1)}) fusion(f32[512,1024]{1,0:T(8,128)S(1)} %get-tuple-element.143, f32[3,512]{1,0:T(4,128)S(1)} %get-tuple-element.140, f32[3,1024]{1,0:T(4,128)S(1)} %get-tuple-element.168, f32[512,1024]{1,0:T(8,128)S(1)} %get-tuple-element.144, ...), kind=kLoop, calls=%fused_computation.8.clone.1 | loop fusion | flops 12579840 | bytes 4243456 | tf_op jit(solution)/shard_map/while/body/eval_jaxpr/reduce_sum | solution.py:37
  85.5 1.1 broadcast_subtract_fusion.3
  86.6 2.1 %fusion.17 = (f32[512,1024]{1,0:T(8,128)S(1)}, f32[512,1024]{1,0:T(8,128)S(1)}) fusion(f32[3,512,1024]{2,1,0:T(8,128)S(1)} %get-tuple-element.141, f32[3,512,1024]{2,1,0:T(8,128)S(1)} %get-tuple-element.142, f32[1024]{0:T(1024)S(1)} %bitcast.47), kind=kLoop, calls=%fused_computation.15.clone.1 | loop fusion | flops 8388608 | bytes 16781312 | tf_op jit(solution)/shard_map/while/body/eval_jaxpr/mul | solution.py:38
  88.7 2.5 %multiply_reduce_fusion.3 = (f32[3,512]{1,0:T(4,128)S(1)}, f32[3,512]{1,0:T(4,128)S(1)}) fusion(f32[512,1024]{1,0:T(8,128)S(1)} %get-tuple-element.143, f32[3,512]{1,0:T(4,128)S(1)} %get-tuple-element.140, f32[3,1024]{1,0:T(4,128)S(1)} %get-tuple-element.168, f32[512,1024]{1,0:T(8,128)S(1)} %get-tuple-element.144, ...), kind=kLoop, calls=%fused_computation.8.clone.1 | loop fusion | flops 12579840 | bytes 4243456 | tf_op jit(solution)/shard_map/while/body/eval_jaxpr/reduce_sum | solution.py:37
  91.2 0.6 copy-done.2
  91.9 1.4 gather_fusion.1
  93.3 0.2 copy.79
  93.5 0.2 copy.83
  93.8 0.7 gather_fusion.2
  94.6 0.7 gather_fusion
  95.4 53.7 %reduce-scatter.2.cloned.1.call-done = f32[6,256]{1,0:T(8,128)} async-done(((f32[6,4096]{1,0:T(8,128)}), f32[6,256]{1,0:T(8,128)}) %reduce-scatter.2.cloned.1.call-update) | async-done | bytes 6160 | tf_op jit(solution)/shard_map/reduce_scatter | solution.py:72
  149.1 0.8 fusion.10
  149.9 0.7 select_bitcast_fusion
  150.6 0.1 copy.86
  150.7 1.4 scatter_fusion.1
  152.1 0.8 copy.88
  153.1 1.4 scatter_fusion
  154.4 0.8 copy.87
  155.3 1.3 maximum_select_fusion
  (35 shorter events, 0.6 us)
Async XLA Ops:
  7.2 142.0 %reduce-scatter.2.cloned.1.call-start = ((), (), s32[]{:S(2)}) async-start(), calls=%async_computation.1 | async-start | bytes 139264 | tf_op jit(solution)/shard_map/reduce_scatter | solution.py:72
  12.6 32.9 %copy-start.3 = (f32[1024]{0:T(1024)S(1)}, f32[1024]{0:T(1024)}, u32[]{:S(2)}) copy-start(f32[1024]{0:T(1024)} %param.11) | copy-start | bytes 12292
  45.5 47.8 %copy-start = (f32[6,1024]{1,0:T(8,128)S(1)}, f32[6,1024]{1,0:T(8,128)}, u32[]{:S(2)}) copy-start(f32[6,1024]{1,0:T(8,128)} %param.10) | copy-start | bytes 73732
  45.5 48.1 %copy-start.1 = (f32[6,1024]{1,0:T(8,128)S(1)}, f32[6,1024]{1,0:T(8,128)}, u32[]{:S(2)}) copy-start(f32[6,1024]{1,0:T(8,128)} %param.9) | copy-start | bytes 73732
  91.2 0.6 copy-start.2
Sparse Core Ops, SparseCore 0:
  92.0 57.0 reduce-scatter.1
where the time goes:
time: 164 us; the launch traced here: 163 us
  waiting for transfers between devices  53.7 us (33%)
  other arithmetic  50.4 us (31%)
  blocking collectives  32.3 us (20%)
  between operations  14.8 us (9%)
  local copies, waits for them, and re-layouts  11.8 us (7%)
    reduce_scatter x1, waiting for transfers between devices, per_device(): fresh = lax.psum_scatter(every_slot, 'ja', scatter_dimension=1, tiled=True)  53.7 us
    all_gather x1, blocking collectives, per_device(): lax.all_gather(targets, 'ja', axis=1, tiled=True)  32.3 us
    reduce_sum x8, other arithmetic, pair_block(): accel_part = jnp.sum(weight[None] * delta_x, axis=2)  20 us
    mul x8, other arithmetic, pair_block(): radial[None] * delta_x  16.6 us
    sub x8, other arithmetic, pair_block(): delta_v = sources[3:6, None, :] - targets[3:6, :, None]  8.53 us
  transfers between devices with their start and end apart: 1, of which 1 were waited for; matrix products, arithmetic and copies ran while one was open for 2% of the time, Pallas kernels for 0%

commit v1 on v0

v1 whole, which is shorter than its diff:
```python
import functools

import jax
import jax.numpy as jnp
from jax import lax
from jax.experimental import pallas as pl
from jax.experimental.pallas import tpu as pltpu
from jax.sharding import PartitionSpec as P

A_DEV = 128
CAPACITY = 2 * A_DEV
LANES = 128

soft_sq = 0.01
base_step = 2.0


def step_length(level):
    length = jnp.full(level.shape, base_step, jnp.float32)
    for bit, factor in ((1, 0.5), (2, 0.25), (4, 0.0625)):
        length = length * jnp.where((level & bit) != 0, jnp.float32(factor), jnp.float32(1.0))
    return length


def lane_gather(values, lane):
    return jnp.take_along_axis(values, lane, axis=1)


def gather_from_stars(values, ids):
    group, lane = ids // LANES, ids % LANES
    out = jnp.zeros((8, LANES), jnp.float32)
    for g in range(values.shape[1] // LANES):
        part = lane_gather(values[:, g * LANES : (g + 1) * LANES], lane)
        out = jnp.where(group == g, part, out)
    return out


def correct(old_pv, old_aj, fresh, step_len):
    half = 0.5 * step_len
    twelfth = step_len * step_len * jnp.float32(1.0 / 12.0)
    velocity = (
        old_pv[3:6] + half * (old_aj[0:3] + fresh[0:3]) + twelfth * (old_aj[3:6] - fresh[3:6])
    )
    position = old_pv[0:3] + half * (old_pv[3:6] + velocity) + twelfth * (old_aj[0:3] - fresh[0:3])
    return position, velocity


def kernel(
    n, counts_ref, pv_ref, aj_ref, mass_ref, phase_ref, level_ref, order_ref,
    npv_ref, naj_ref, state_ref,
    srcs, tgts, res, wide, acc, old, slot_row,
    tgt_send, tgt_recv, src_send, src_recv, relay_send, res_send, res_recv,
):
    me = lax.axis_index("ja")
    core, chip, chips = me % 2, me // 2, n // 2
    sibling = me + 1 - 2 * core
    stars = pv_ref.shape[1]

    barrier = pltpu.get_barrier_semaphore()

    def greet(k, carry):
        pl.semaphore_signal(barrier, inc=1, device_id={"ja": (me + k) % n})
        return carry

    lax.fori_loop(1, n, greet, 0)

    count = counts_ref[0]
    order = order_ref[0:1, 0:CAPACITY]
    slots = lax.broadcasted_iota(jnp.int32, (CAPACITY, LANES), 0)
    column = jnp.transpose(jnp.broadcast_to(order.astype(jnp.float32), (8, CAPACITY)))[:, 0:1]
    column = jnp.broadcast_to(column, (CAPACITY, LANES)).astype(jnp.int32)
    column = jnp.where(slots < count, column, -1)
    lanes = lax.broadcasted_iota(jnp.int32, (CAPACITY, LANES), 1)
    for g in range(stars // LANES):
        found = jnp.where(column == lanes + g * LANES, slots, -1)
        slot_row[0:1, g * LANES : (g + 1) * LANES] = jnp.max(found, axis=0, keepdims=True)
    active = slot_row[0:1, :] >= 0

    step_len = step_length(level_ref[...])
    age = step_len * jnp.where(active, jnp.float32(1.0), phase_ref[...])
    half_sq = 0.5 * age * age
    sixth_cube = age * age * age * jnp.float32(1.0 / 6.0)
    pos, vel = pv_ref[0:3, :], pv_ref[3:6, :]
    acl, jrk = aj_ref[0:3, :], aj_ref[3:6, :]
    srcs[me, 0:3, :] = pos + age * vel + half_sq * acl + sixth_cube * jrk
    srcs[me, 3:6, :] = vel + age * acl + half_sq * jrk
    srcs[me, 6:7, :] = mass_ref[...]
    srcs[me, 7:8, :] = step_len

    predicted = srcs[me]
    row = lax.broadcasted_iota(jnp.int32, (8, LANES), 0)
    for h in range(2):
        span = slice(h * LANES, (h + 1) * LANES)
        ids = jnp.broadcast_to(order_ref[0:1, span], (8, LANES))
        got = gather_from_stars(predicted, ids)
        tgts[me, :, span] = jnp.where(row == 6, count.astype(jnp.float32), got)
        old[2, :, span] = got
    tgt_copy = lambda k, o, peer: pltpu.make_async_remote_copy(
        src_ref=tgts.at[o], dst_ref=tgts.at[o], send_sem=tgt_send.at[k], recv_sem=tgt_recv.at[o],
        device_id={"ja": peer},
    )
    src_copy = lambda k, o, peer: pltpu.make_async_remote_copy(
        src_ref=srcs.at[o], dst_ref=srcs.at[o], send_sem=src_send.at[k], recv_sem=src_recv.at[o],
        device_id={"ja": peer},
    )
    relay_copy = lambda k, o: pltpu.make_async_remote_copy(
        src_ref=srcs.at[o], dst_ref=srcs.at[o], send_sem=relay_send.at[k], recv_sem=src_recv.at[o],
        device_id={"ja": sibling},
    )
    res_copy = lambda k, o, peer: pltpu.make_async_remote_copy(
        src_ref=res.at[o], dst_ref=res.at[o], send_sem=res_send.at[k], recv_sem=res_recv.at[o],
        device_id={"ja": peer},
    )

    pl.semaphore_wait(barrier, n - 1)

    def send_targets(k, carry):
        tgt_copy(k, me, (me + k) % n).start()
        return carry

    lax.fori_loop(1, n, send_targets, 0)
    src_copy(0, me, sibling).start()

    def send_sources(j, carry):
        src_copy(j, me, 2 * ((chip + j) % chips) + core).start()
        return carry

    lax.fori_loop(1, chips, send_sources, 0)

    pv_pad = jnp.concatenate([pv_ref[...], jnp.zeros((2, stars), jnp.float32)], axis=0)
    aj_pad = jnp.concatenate([aj_ref[...], jnp.zeros((2, stars), jnp.float32)], axis=0)
    for h in range(2):
        span = slice(h * LANES, (h + 1) * LANES)
        ids = jnp.broadcast_to(order_ref[0:1, span], (8, LANES))
        old[0, :, span] = gather_from_stars(pv_pad, ids)
        old[1, :, span] = gather_from_stars(aj_pad, ids)
    acc[...] = jnp.zeros_like(acc)

    def arrive_targets(k, carry):
        o = (me + n - k) % n
        tgt_copy(k, o, (me + k) % n).wait_recv()
        return carry

    lax.fori_loop(1, n, arrive_targets, 0)

    lane8 = lax.broadcasted_iota(jnp.int32, (8, LANES), 1)

    def pack(o, carry):
        place, mine, packed = carry
        low, high = tgts[o, :, 0:LANES], tgts[o, :, LANES:CAPACITY]
        number = jnp.broadcast_to(low[6:7, :], (8, LANES)).astype(jnp.int32)
        lane = place & (LANES - 1)
        chosen = jnp.where(place < LANES, lane_gather(low, lane), lane_gather(high, lane))
        packed = jnp.where((place >= 0) & (place < number), chosen, packed)
        mine = jnp.where(o == me, 2 * lane8 + me * A_DEV - place, mine)
        return place - number, mine, packed

    _, mine, packed = lax.fori_loop(
        0, n, pack, (lane8 + me * A_DEV, lane8, jnp.zeros((8, LANES), jnp.float32))
    )
    upright = jnp.transpose(packed)
    for c in range(6):
        wide[c, :, :] = jnp.broadcast_to(upright[:, c : c + 1], (A_DEV, LANES))

    def pairs(o):
        def tile(t, carry):
            rows = pl.ds(pl.multiple_of(t * 16, 16), 16)
            at = [wide[c, rows, :] for c in range(6)]
            sums = [acc[c, rows, :] for c in range(9)]
            for g in range(stars // LANES):
                span = slice(g * LANES, (g + 1) * LANES)
                s = [jnp.broadcast_to(srcs[o, c : c + 1, span], (16, LANES)) for c in range(7)]
                dx = [s[c] - at[c] for c in range(3)]
                dv = [s[c + 3] - at[c + 3] for c in range(3)]
                dist_sq = soft_sq + dx[0] * dx[0] + dx[1] * dx[1] + dx[2] * dx[2]
                inverse = lax.rsqrt(dist_sq)
                inverse_sq = inverse * inverse
                weight = s[6] * inverse * inverse_sq
                radial = (dx[0] * dv[0] + dx[1] * dv[1] + dx[2] * dv[2]) * inverse_sq * weight
                for c in range(3):
                    sums[c] = sums[c] + weight * dx[c]
                    sums[c + 3] = sums[c + 3] + weight * dv[c]
                    sums[c + 6] = sums[c + 6] + radial * dx[c]
            for c in range(9):
                acc[c, rows, :] = sums[c]
            return carry

        lax.fori_loop(0, A_DEV // 16, tile, 0)

    pairs(me)

    def visit(j, carry):
        direct = 2 * ((chip + chips - j) % chips) + core
        src_copy(j, direct, direct).wait_recv()
        relay_copy(j, direct).start()
        pairs(direct)
        passed = 2 * ((chip + chips - j + 1) % chips) + 1 - core
        src_copy(0, passed, sibling).wait_recv()
        pairs(passed)
        return carry

    lax.fori_loop(1, chips, visit, 0)
    last = 2 * ((chip + 1) % chips) + 1 - core
    src_copy(0, last, sibling).wait_recv()
    pairs(last)

    ones = jnp.ones((8, LANES), jnp.float32)

    def total(c):
        return lax.dot_general(
            ones, acc[c], (((1,), (1,)), ((), ())), precision=lax.Precision.HIGHEST,
            preferred_element_type=jnp.float32,
        )

    fresh = jnp.zeros((8, LANES), jnp.float32)
    for c in range(3):
        fresh = jnp.where(row == c, total(c), fresh)
        fresh = jnp.where(row == c + 3, total(c + 3) - 3.0 * total(c + 6), fresh)
    res[me] = fresh

    def send_results(k, carry):
        res_copy(k, me, (me + k) % n).start()
        return carry

    lax.fori_loop(1, n, send_results, 0)

    def arrive_results(k, carry):
        o = (me + n - k) % n
        res_copy(k, o, (me + k) % n).wait_recv()
        return carry

    lax.fori_loop(1, n, arrive_results, 0)

    where = [mine + h * LANES for h in range(2)]

    def unpack(o, carry):
        block = res[o]
        return tuple(
            jnp.where(w // LANES == o, lane_gather(block, w % LANES), kept)
            for w, kept in zip(where, carry)
        )

    blank = jnp.zeros((8, LANES), jnp.float32)
    parts = lax.fori_loop(0, n, unpack, (blank, blank))

    for h in range(2):
        span = slice(h * LANES, (h + 1) * LANES)
        live = lane8[0:3] + h * LANES < count
        new_x, new_v = correct(old[0, :, span], old[1, :, span], parts[h], old[2, 7:8, span])
        state_ref[0:3, span] = jnp.where(live, new_x, 0.0)
        state_ref[3:6, span] = jnp.where(live, new_v, 0.0)
        state_ref[6:9, span] = jnp.where(live, parts[h][0:3], 0.0)
        state_ref[9:12, span] = jnp.where(live, parts[h][3:6], 0.0)
    for g in range(stars // LANES):
        span = slice(g * LANES, (g + 1) * LANES)
        slot = jnp.broadcast_to(slot_row[0:1, span], (8, LANES))
        lane = slot & (LANES - 1)
        star = jnp.where(slot < LANES, lane_gather(parts[0], lane), lane_gather(parts[1], lane))
        on = slot[0:3] >= 0
        new_x, new_v = correct(pv_ref[:, span], aj_ref[:, span], star, srcs[me, 7:8, span])
        npv_ref[0:3, span] = jnp.where(on, new_x, pv_ref[0:3, span])
        npv_ref[3:6, span] = jnp.where(on, new_v, pv_ref[3:6, span])
        naj_ref[0:3, span] = jnp.where(on, star[0:3], aj_ref[0:3, span])
        naj_ref[3:6, span] = jnp.where(on, star[3:6], aj_ref[3:6, span])

    def drain(k, carry):
        tgt_copy(k, me, (me + k) % n).wait_send()
        res_copy(k, me, (me + k) % n).wait_send()
        return carry

    lax.fori_loop(1, n, drain, 0)
    src_copy(0, me, sibling).wait_send()

    def drain_sources(j, carry):
        direct = 2 * ((chip + chips - j) % chips) + core
        src_copy(j, me, direct).wait_send()
        relay_copy(j, direct).wait_send()
        return carry

    lax.fori_loop(1, chips, drain_sources, 0)


def per_device(n, pos_vel, acc_jerk, star_mass, step_phase, step_level, counts, star_order):
    stars = pos_vel.shape[1]
    vmem = pl.BlockSpec(memory_space=pltpu.VMEM)
    row = lambda a: a.reshape(1, stars)
    return pl.pallas_call(
        functools.partial(kernel, n),
        out_shape=(
            jax.ShapeDtypeStruct((6, stars), jnp.float32),
            jax.ShapeDtypeStruct((6, stars), jnp.float32),
            jax.ShapeDtypeStruct((12, CAPACITY), jnp.float32),
        ),
        in_specs=[pl.BlockSpec(memory_space=pltpu.SMEM)] + [vmem] * 6,
        out_specs=(vmem, vmem, vmem),
        scratch_shapes=[
            pltpu.VMEM((n, 8, stars), jnp.float32),
            pltpu.VMEM((n, 8, CAPACITY), jnp.float32),
            pltpu.VMEM((n, 8, A_DEV), jnp.float32),
            pltpu.VMEM((6, A_DEV, LANES), jnp.float32),
            pltpu.VMEM((9, A_DEV, LANES), jnp.float32),
            pltpu.VMEM((3, 8, CAPACITY), jnp.float32),
            pltpu.VMEM((8, stars), jnp.int32),
            pltpu.SemaphoreType.DMA((n,)),
            pltpu.SemaphoreType.DMA((n,)),
            pltpu.SemaphoreType.DMA((n,)),
            pltpu.SemaphoreType.DMA((n,)),
            pltpu.SemaphoreType.DMA((n,)),
            pltpu.SemaphoreType.DMA((n,)),
            pltpu.SemaphoreType.DMA((n,)),
        ],
        compiler_params=pltpu.CompilerParams(collective_id=0, has_side_effects=True),
        name="block_step",
    )(counts, pos_vel, acc_jerk, row(star_mass), row(step_phase), row(step_level), star_order)


def solution(mesh):
    n = mesh.shape["ja"]
    in_specs = (
        P(None, ("runs", "ja")),
        P(None, ("runs", "ja")),
        P(("runs", "ja")),
        P(("runs", "ja")),
        P(("runs", "ja")),
        P(("runs", "ja")),
        P(("runs", "ja"), None),
    )
    out_specs = (P(None, ("runs", "ja")), P(None, ("runs", "ja")), P(None, ("runs", "ja")))
    return jax.shard_map(
        functools.partial(per_device, n),
        mesh=mesh, in_specs=in_specs, out_specs=out_specs, check_vma=False,
    )
```

time: 164 us -> 39.7 us (0.24)
  waiting for transfers between devices: 53.7 us -> 0 us
  other arithmetic: 50.4 us -> 0 us
  Pallas kernels: 0 us -> 35.3 us
  blocking collectives: 32.3 us -> 0 us
  between operations: 14.8 us -> 1.3 us
  local copies, waits for them, and re-layouts: 11.8 us -> 2.72 us
    reduce_scatter x1 -> x0, waiting for transfers between devices: 53.7 us -> none  [per_device(): fresh = lax.psum_scatter(every_slot, 'ja', scatter_dimension=1, tiled=True)]
    pallas_call x0 -> x1, Pallas kernels: none -> 35.3 us  [per_device(): pl.pallas_call(functools.partial(kernel, n), out_shape=(jax.ShapeDtypeStr...]
    all_gather x1 -> x0, blocking collectives: 32.3 us -> none  [per_device(): lax.all_gather(targets, 'ja', axis=1, tiled=True)]
    reduce_sum x8 -> x0, other arithmetic: 20 us -> none  [pair_block(): accel_part = jnp.sum(weight[None] * delta_x, axis=2)]
    mul x10 -> x0, other arithmetic: 17.4 us -> none  [the longest x8 16.6 us: pair_block(): radial[None] * delta_x]
    sub x8 -> x0, other arithmetic: 8.53 us -> none  [pair_block(): delta_v = sources[3:6, None, :] - targets[3:6, :, None]]
    scatter x3 -> x0, local copies, waits for them, and re-layouts: 4.15 us -> none  [the longest x1 1.41 us: per_device(): jnp.zeros((per_owner,), jnp.float32).at[slot_ids]]
    gather x6 -> x0, local copies, waits for them, and re-layouts: 3.73 us -> none  [the longest x1 1.37 us: per_device(): corrected = correct(old_pv, old_aj, fresh, step_len[slot_ids])]
  transfers between devices with their start and end apart: 1 -> 0, of which waited for: 1 -> 0; matrix products, arithmetic and copies ran while one was open for 2% -> 0% of each run, Pallas kernels for 0% -> 0%
where the time goes in v1:
time: 39.7 us; the launch traced here: 39.3 us
  Pallas kernels  35.3 us (89%)
  local copies, waits for them, and re-layouts  2.72 us (7%)
  between operations  1.3 us (3%)
    pallas_call x1, Pallas kernels, per_device(): pl.pallas_call(functools.partial(kernel, n), out_shape=(jax.ShapeDtypeStr...  35.3 us
    unnamed x7, local copies, waits for them, and re-layouts  2.72 us

profile of v1, /device:TPU:0, one launch (start us, length us, event | category | flops | bytes accessed | tf_op | source)
XLA Modules:
  0.0 39.3 jit_solution(8780120869444377230)
XLA Ops:
  1.3 35.3 %block_step.1 = (f32[6,1024]{1,0:T(8,128)}, f32[6,1024]{1,0:T(8,128)}, f32[12,256]{1,0:T(8,128)}) custom-call(s32[1]{0:T(128)S(6)} %copy.13.counts_ref, f32[6,1024]{1,0:T(8,128)} %pv_ref.1, f32[6,1024]{1,0:T(8,128)} %aj_ref.1, f32[1,1024]{1,0:T(1,128)} %bitcast.3, f32[1,1024]{1,0:T(1,128)} %bitcast.4, s32[1,1024]{1,0:T(1,128)} %bitcast.5, s32[1,1024]{1,0:T(1,128)} %order_ref.1), custom_call_target="tpu_custom_call" | custom-call | tf_op jit(solution)/shard_map/block_step/pallas_call | solution.py:287
  36.6 0.0 copy-start
  36.6 1.4 %copy.14 = f32[6,1024]{1,0:T(8,128)} copy(f32[6,1024]{1,0:T(8,128)} %get-tuple-element.6) | data formatting | bytes 49152
  38.0 0.0 copy-done
  38.0 0.0 copy-start.1
  38.0 0.6 %copy.15 = f32[6,1024]{1,0:T(8,128)} copy(f32[6,1024]{1,0:T(8,128)S(1)} %copy-done) | data formatting | bytes 49152
  38.6 0.1 copy-done.1
  38.7 0.6 %copy.16 = f32[12,256]{1,0:T(8,128)} copy(f32[12,256]{1,0:T(8,128)S(1)} %copy-done.1) | data formatting | bytes 24576
Async XLA Ops:
  36.6 1.4 %copy-start = (f32[6,1024]{1,0:T(8,128)S(1)}, f32[6,1024]{1,0:T(8,128)}, u32[]{:S(2)}) copy-start(f32[6,1024]{1,0:T(8,128)} %get-tuple-element.7) | copy-start | bytes 73732
  38.0 0.7 %copy-start.1 = (f32[12,256]{1,0:T(8,128)S(1)}, f32[12,256]{1,0:T(8,128)}, u32[]{:S(2)}) copy-start(f32[12,256]{1,0:T(8,128)} %get-tuple-element.8) | copy-start | bytes 36868

commit v2 on v1

--- a/solution.py
+++ b/solution.py
@@ -64,12 +64,12 @@
 
     lax.fori_loop(1, n, greet, 0)
 
-    count = counts_ref[0]
+    count = jnp.broadcast_to(counts_ref[...], (8, LANES))
     order = order_ref[0:1, 0:CAPACITY]
     slots = lax.broadcasted_iota(jnp.int32, (CAPACITY, LANES), 0)
     column = jnp.transpose(jnp.broadcast_to(order.astype(jnp.float32), (8, CAPACITY)))[:, 0:1]
     column = jnp.broadcast_to(column, (CAPACITY, LANES)).astype(jnp.int32)
-    column = jnp.where(slots < count, column, -1)
+    column = jnp.where(slots < jnp.broadcast_to(count[0:1], (CAPACITY, LANES)), column, -1)
     lanes = lax.broadcasted_iota(jnp.int32, (CAPACITY, LANES), 1)
     for g in range(stars // LANES):
         found = jnp.where(column == lanes + g * LANES, slots, -1)
@@ -96,21 +96,25 @@
         tgts[me, :, span] = jnp.where(row == 6, count.astype(jnp.float32), got)
         old[2, :, span] = got
     tgt_copy = lambda k, o, peer: pltpu.make_async_remote_copy(
-        src_ref=tgts.at[o], dst_ref=tgts.at[o], send_sem=tgt_send.at[k], recv_sem=tgt_recv.at[o],
+        src_ref=tgts.at[o], dst_ref=tgts.at[o], send_sem=tgt_send, recv_sem=tgt_recv,
         device_id={"ja": peer},
     )
     src_copy = lambda k, o, peer: pltpu.make_async_remote_copy(
-        src_ref=srcs.at[o], dst_ref=srcs.at[o], send_sem=src_send.at[k], recv_sem=src_recv.at[o],
+        src_ref=srcs.at[o], dst_ref=srcs.at[o], send_sem=src_send, recv_sem=src_recv.at[o],
         device_id={"ja": peer},
     )
     relay_copy = lambda k, o: pltpu.make_async_remote_copy(
-        src_ref=srcs.at[o], dst_ref=srcs.at[o], send_sem=relay_send.at[k], recv_sem=src_recv.at[o],
+        src_ref=srcs.at[o], dst_ref=srcs.at[o], send_sem=relay_send, recv_sem=src_recv.at[o],
         device_id={"ja": sibling},
     )
     res_copy = lambda k, o, peer: pltpu.make_async_remote_copy(
-        src_ref=res.at[o], dst_ref=res.at[o], send_sem=res_send.at[k], recv_sem=res_recv.at[o],
+        src_ref=res.at[o], dst_ref=res.at[o], send_sem=res_send, recv_sem=res_recv,
         device_id={"ja": peer},
     )
+
+    def await_all(ref, number, sem):
+        part = ref.at[pl.ds(0, number)]
+        pltpu.make_async_copy(part, part, sem).wait()
 
     pl.semaphore_wait(barrier, n - 1)
 
@@ -136,12 +140,7 @@
         old[1, :, span] = gather_from_stars(aj_pad, ids)
     acc[...] = jnp.zeros_like(acc)
 
-    def arrive_targets(k, carry):
-        o = (me + n - k) % n
-        tgt_copy(k, o, (me + k) % n).wait_recv()
-        return carry
-
-    lax.fori_loop(1, n, arrive_targets, 0)
+    await_all(tgts, n - 1, tgt_recv)
 
     lane8 = lax.broadcasted_iota(jnp.int32, (8, LANES), 1)
 
@@ -155,8 +154,16 @@
         mine = jnp.where(o == me, 2 * lane8 + me * A_DEV - place, mine)
         return place - number, mine, packed
 
+    def by_four(step):
+        def four(b, carry):
+            for k in range(4):
+                carry = step(4 * b + k, carry)
+            return carry
+
+        return four
+
     _, mine, packed = lax.fori_loop(
-        0, n, pack, (lane8 + me * A_DEV, lane8, jnp.zeros((8, LANES), jnp.float32))
+        0, n // 4, by_four(pack), (lane8 + me * A_DEV, lane8, jnp.zeros((8, LANES), jnp.float32))
     )
     upright = jnp.transpose(packed)
     for c in range(6):
@@ -176,11 +183,12 @@
                 inverse = lax.rsqrt(dist_sq)
                 inverse_sq = inverse * inverse
                 weight = s[6] * inverse * inverse_sq
-                radial = (dx[0] * dv[0] + dx[1] * dv[1] + dx[2] * dv[2]) * inverse_sq * weight
+                radial = (dx[0] * dv[0] + dx[1] * dv[1] + dx[2] * dv[2]) * inverse_sq
                 for c in range(3):
-                    sums[c] = sums[c] + weight * dx[c]
+                    pull = weight * dx[c]
+                    sums[c] = sums[c] + pull
                     sums[c + 3] = sums[c + 3] + weight * dv[c]
-                    sums[c + 6] = sums[c + 6] + radial * dx[c]
+                    sums[c + 6] = sums[c + 6] + radial * pull
             for c in range(9):
                 acc[c, rows, :] = sums[c]
             return carry
@@ -204,18 +212,12 @@
     src_copy(0, last, sibling).wait_recv()
     pairs(last)
 
-    ones = jnp.ones((8, LANES), jnp.float32)
-
-    def total(c):
-        return lax.dot_general(
-            ones, acc[c], (((1,), (1,)), ((), ())), precision=lax.Precision.HIGHEST,
-            preferred_element_type=jnp.float32,
-        )
-
-    fresh = jnp.zeros((8, LANES), jnp.float32)
-    for c in range(3):
-        fresh = jnp.where(row == c, total(c), fresh)
-        fresh = jnp.where(row == c + 3, total(c + 3) - 3.0 * total(c + 6), fresh)
+    columns = lax.broadcasted_iota(jnp.int32, (A_DEV, LANES), 1)
+    upright = jnp.zeros((A_DEV, LANES), jnp.float32)
+    for c in range(6):
+        part = acc[c] if c < 3 else acc[c] - 3.0 * acc[c + 3]
+        upright = jnp.where(columns == c, jnp.sum(part, axis=1, keepdims=True), upright)
+    fresh = jnp.transpose(upright)[0:8]
     res[me] = fresh
 
     def send_results(k, carry):
@@ -224,12 +226,7 @@
 
     lax.fori_loop(1, n, send_results, 0)
 
-    def arrive_results(k, carry):
-        o = (me + n - k) % n
-        res_copy(k, o, (me + k) % n).wait_recv()
-        return carry
-
-    lax.fori_loop(1, n, arrive_results, 0)
+    await_all(res, n - 1, res_recv)
 
     where = [mine + h * LANES for h in range(2)]
 
@@ -241,11 +238,11 @@
         )
 
     blank = jnp.zeros((8, LANES), jnp.float32)
-    parts = lax.fori_loop(0, n, unpack, (blank, blank))
+    parts = lax.fori_loop(0, n // 4, by_four(unpack), (blank, blank))
 
     for h in range(2):
         span = slice(h * LANES, (h + 1) * LANES)
-        live = lane8[0:3] + h * LANES < count
+        live = lane8[0:3] + h * LANES < count[0:3]
         new_x, new_v = correct(old[0, :, span], old[1, :, span], parts[h], old[2, 7:8, span])
         state_ref[0:3, span] = jnp.where(live, new_x, 0.0)
         state_ref[3:6, span] = jnp.where(live, new_v, 0.0)
@@ -263,21 +260,10 @@
         naj_ref[0:3, span] = jnp.where(on, star[0:3], aj_ref[0:3, span])
         naj_ref[3:6, span] = jnp.where(on, star[3:6], aj_ref[3:6, span])
 
-    def drain(k, carry):
-        tgt_copy(k, me, (me + k) % n).wait_send()
-        res_copy(k, me, (me + k) % n).wait_send()
-        return carry
-
-    lax.fori_loop(1, n, drain, 0)
-    src_copy(0, me, sibling).wait_send()
-
-    def drain_sources(j, carry):
-        direct = 2 * ((chip + chips - j) % chips) + core
-        src_copy(j, me, direct).wait_send()
-        relay_copy(j, direct).wait_send()
-        return carry
-
-    lax.fori_loop(1, chips, drain_sources, 0)
+    await_all(tgts, n - 1, tgt_send)
+    await_all(res, n - 1, res_send)
+    await_all(srcs, chips, src_send)
+    await_all(srcs, chips - 1, relay_send)
 
 
 def per_device(n, pos_vel, acc_jerk, star_mass, step_phase, step_level, counts, star_order):
@@ -287,11 +273,11 @@
     return pl.pallas_call(
         functools.partial(kernel, n),
         out_shape=(
-            jax.ShapeDtypeStruct((6, stars), jnp.float32),
-            jax.ShapeDtypeStruct((6, stars), jnp.float32),
-            jax.ShapeDtypeStruct((12, CAPACITY), jnp.float32),
+            pltpu.VMEM((6, stars), jnp.float32),
+            pltpu.VMEM((6, stars), jnp.float32),
+            pltpu.VMEM((12, CAPACITY), jnp.float32),
         ),
-        in_specs=[pl.BlockSpec(memory_space=pltpu.SMEM)] + [vmem] * 6,
+        in_specs=[vmem] * 7,
         out_specs=(vmem, vmem, vmem),
         scratch_shapes=[
             pltpu.VMEM((n, 8, stars), jnp.float32),
@@ -301,17 +287,17 @@
             pltpu.VMEM((9, A_DEV, LANES), jnp.float32),
             pltpu.VMEM((3, 8, CAPACITY), jnp.float32),
             pltpu.VMEM((8, stars), jnp.int32),
+            pltpu.SemaphoreType.DMA,
+            pltpu.SemaphoreType.DMA,
+            pltpu.SemaphoreType.DMA,
             pltpu.SemaphoreType.DMA((n,)),
-            pltpu.SemaphoreType.DMA((n,)),
-            pltpu.SemaphoreType.DMA((n,)),
-            pltpu.SemaphoreType.DMA((n,)),
-            pltpu.SemaphoreType.DMA((n,)),
-            pltpu.SemaphoreType.DMA((n,)),
-            pltpu.SemaphoreType.DMA((n,)),
+            pltpu.SemaphoreType.DMA,
+            pltpu.SemaphoreType.DMA,
+            pltpu.SemaphoreType.DMA,
         ],
         compiler_params=pltpu.CompilerParams(collective_id=0, has_side_effects=True),
         name="block_step",
-    )(counts, pos_vel, acc_jerk, row(star_mass), row(step_phase), row(step_level), star_order)
+    )(counts.reshape(1, 1), pos_vel, acc_jerk, row(star_mass), row(step_phase), row(step_level), star_order)
 
 
 def solution(mesh):

time: 39.7 us -> 34.8 us (0.88)
  Pallas kernels: 35.3 us -> 31.5 us
  local copies, waits for them, and re-layouts: 2.72 us -> 1.84 us
    pallas_call x1, Pallas kernels: 35.3 us -> 31.5 us  [per_device(): pl.pallas_call(functools.partial(kernel, n), out_shape=(pltpu.VMEM((6, st...]
    unnamed x7 -> x3, local copies, waits for them, and re-layouts: 2.72 us -> 1.84 us
where the time goes in v2:
time: 34.8 us; the launch traced here: 34.6 us
  Pallas kernels  31.5 us (91%)
  local copies, waits for them, and re-layouts  1.84 us (5%)
  between operations  1.29 us (4%)
    pallas_call x1, Pallas kernels, per_device(): pl.pallas_call(functools.partial(kernel, n), out_shape=(pltpu.VMEM((6, st...  31.5 us
    unnamed x3, local copies, waits for them, and re-layouts  1.84 us

profile of v2, /device:TPU:0, one launch (start us, length us, event | category | flops | bytes accessed | tf_op | source)
XLA Modules:
  0.0 34.6 jit_solution(17897721167550203050)
XLA Ops:
  1.3 31.5 %block_step.1 = (f32[6,1024]{1,0:T(8,128)S(1)}, f32[6,1024]{1,0:T(8,128)S(1)}, f32[12,256]{1,0:T(8,128)S(1)}) custom-call(s32[1,1]{1,0:T(1,128)} %bitcast.4.counts_ref, f32[6,1024]{1,0:T(8,128)} %pv_ref.1, f32[6,1024]{1,0:T(8,128)} %aj_ref.1, f32[1,1024]{1,0:T(1,128)} %bitcast.5, f32[1,1024]{1,0:T(1,128)} %bitcast.6, s32[1,1024]{1,0:T(1,128)} %bitcast.7, ...), custom_call_target="tpu_custom_call" | custom-call | tf_op jit(solution)/shard_map/block_step/pallas_call | solution.py:273
  32.8 0.6 %copy.13 = f32[6,1024]{1,0:T(8,128)} copy(f32[6,1024]{1,0:T(8,128)S(1)} %get-tuple-element.3) | data formatting | bytes 49152
  33.4 0.6 %copy.15 = f32[12,256]{1,0:T(8,128)} copy(f32[12,256]{1,0:T(8,128)S(1)} %get-tuple-element.5) | data formatting | bytes 24576
  34.0 0.6 %copy.14 = f32[6,1024]{1,0:T(8,128)} copy(f32[6,1024]{1,0:T(8,128)S(1)} %get-tuple-element.4) | data formatting | bytes 49152

commit v3 on v2

--- a/solution.py
+++ b/solution.py
@@ -96,7 +96,7 @@
         tgts[me, :, span] = jnp.where(row == 6, count.astype(jnp.float32), got)
         old[2, :, span] = got
     tgt_copy = lambda k, o, peer: pltpu.make_async_remote_copy(
-        src_ref=tgts.at[o], dst_ref=tgts.at[o], send_sem=tgt_send, recv_sem=tgt_recv,
+        src_ref=tgts.at[o, pl.ds(0, 7)], dst_ref=tgts.at[o, pl.ds(0, 7)], send_sem=tgt_send, recv_sem=tgt_recv,
         device_id={"ja": peer},
     )
     src_copy = lambda k, o, peer: pltpu.make_async_remote_copy(
@@ -108,12 +108,12 @@
         device_id={"ja": sibling},
     )
     res_copy = lambda k, o, peer: pltpu.make_async_remote_copy(
-        src_ref=res.at[o], dst_ref=res.at[o], send_sem=res_send, recv_sem=res_recv,
+        src_ref=res.at[o, pl.ds(0, 6)], dst_ref=res.at[o, pl.ds(0, 6)], send_sem=res_send, recv_sem=res_recv,
         device_id={"ja": peer},
     )
 
-    def await_all(ref, number, sem):
-        part = ref.at[pl.ds(0, number)]
+    def await_all(ref, number, sem, rows=8):
+        part = ref.at[pl.ds(0, number), pl.ds(0, rows)]
         pltpu.make_async_copy(part, part, sem).wait()
 
     pl.semaphore_wait(barrier, n - 1)
@@ -140,7 +140,7 @@
         old[1, :, span] = gather_from_stars(aj_pad, ids)
     acc[...] = jnp.zeros_like(acc)
 
-    await_all(tgts, n - 1, tgt_recv)
+    await_all(tgts, n - 1, tgt_recv, 7)
 
     lane8 = lax.broadcasted_iota(jnp.int32, (8, LANES), 1)
 
@@ -193,7 +193,10 @@
                 acc[c, rows, :] = sums[c]
             return carry
 
-        lax.fori_loop(0, A_DEV // 16, tile, 0)
+        def two(b, carry):
+            return tile(2 * b + 1, tile(2 * b, carry))
+
+        lax.fori_loop(0, A_DEV // 32, two, 0)
 
     pairs(me)
 
@@ -226,7 +229,7 @@
 
     lax.fori_loop(1, n, send_results, 0)
 
-    await_all(res, n - 1, res_recv)
+    await_all(res, n - 1, res_recv, 6)
 
     where = [mine + h * LANES for h in range(2)]
 
@@ -260,8 +263,8 @@
         naj_ref[0:3, span] = jnp.where(on, star[0:3], aj_ref[0:3, span])
         naj_ref[3:6, span] = jnp.where(on, star[3:6], aj_ref[3:6, span])
 
-    await_all(tgts, n - 1, tgt_send)
-    await_all(res, n - 1, res_send)
+    await_all(tgts, n - 1, tgt_send, 7)
+    await_all(res, n - 1, res_send, 6)
     await_all(srcs, chips, src_send)
     await_all(srcs, chips - 1, relay_send)
 

time: 34.8 us -> 33.6 us (0.966)
  Pallas kernels: 31.5 us -> 30.3 us
    pallas_call x1, Pallas kernels: 31.5 us -> 30.3 us  [per_device(): pl.pallas_call(functools.partial(kernel, n), out_shape=(pltpu.VMEM((6, st...]
where the time goes in v3:
time: 33.6 us; the launch traced here: 33.4 us
  Pallas kernels  30.3 us (90%)
  local copies, waits for them, and re-layouts  1.84 us (5%)
  between operations  1.29 us (4%)
    pallas_call x1, Pallas kernels, per_device(): pl.pallas_call(functools.partial(kernel, n), out_shape=(pltpu.VMEM((6, st...  30.3 us
    unnamed x3, local copies, waits for them, and re-layouts  1.84 us

profile of v3, /device:TPU:0, one launch (start us, length us, event | category | flops | bytes accessed | tf_op | source)
XLA Modules:
  0.0 33.4 jit_solution(2639834815834261971)
XLA Ops:
  1.3 30.3 %block_step.1 = (f32[6,1024]{1,0:T(8,128)S(1)}, f32[6,1024]{1,0:T(8,128)S(1)}, f32[12,256]{1,0:T(8,128)S(1)}) custom-call(s32[1,1]{1,0:T(1,128)} %bitcast.4.counts_ref, f32[6,1024]{1,0:T(8,128)} %pv_ref.1, f32[6,1024]{1,0:T(8,128)} %aj_ref.1, f32[1,1024]{1,0:T(1,128)} %bitcast.5, f32[1,1024]{1,0:T(1,128)} %bitcast.6, s32[1,1024]{1,0:T(1,128)} %bitcast.7, ...), custom_call_target="tpu_custom_call" | custom-call | tf_op jit(solution)/shard_map/block_step/pallas_call | solution.py:276
  31.6 0.6 %copy.13 = f32[6,1024]{1,0:T(8,128)} copy(f32[6,1024]{1,0:T(8,128)S(1)} %get-tuple-element.3) | data formatting | bytes 49152
  32.2 0.6 %copy.15 = f32[12,256]{1,0:T(8,128)} copy(f32[12,256]{1,0:T(8,128)S(1)} %get-tuple-element.5) | data formatting | bytes 24576
  32.8 0.6 %copy.14 = f32[6,1024]{1,0:T(8,128)} copy(f32[6,1024]{1,0:T(8,128)S(1)} %get-tuple-element.4) | data formatting | bytes 49152

commit v4 on v3

--- a/solution.py
+++ b/solution.py
@@ -193,10 +193,12 @@
                 acc[c, rows, :] = sums[c]
             return carry
 
-        def two(b, carry):
-            return tile(2 * b + 1, tile(2 * b, carry))
-
-        lax.fori_loop(0, A_DEV // 32, two, 0)
+        def four_tiles(b, carry):
+            for k in range(4):
+                tile(4 * b + k, carry)
+            return carry
+
+        lax.fori_loop(0, A_DEV // 64, four_tiles, 0)
 
     pairs(me)
 

time: 33.6 us -> 33.3 us (level)
  no operation moved by 1% of the time
where the time goes in v4:
time: 33.3 us; the launch traced here: 33.1 us
  Pallas kernels  30 us (90%)
  local copies, waits for them, and re-layouts  1.84 us (6%)
  between operations  1.29 us (4%)
    pallas_call x1, Pallas kernels, per_device(): pl.pallas_call(functools.partial(kernel, n), out_shape=(pltpu.VMEM((6, st...  30 us
    unnamed x3, local copies, waits for them, and re-layouts  1.84 us

profile of v4, /device:TPU:0, one launch (start us, length us, event | category | flops | bytes accessed | tf_op | source)
XLA Modules:
  0.0 33.1 jit_solution(7180563346974359116)
XLA Ops:
  1.3 30.0 %block_step.1 = (f32[6,1024]{1,0:T(8,128)S(1)}, f32[6,1024]{1,0:T(8,128)S(1)}, f32[12,256]{1,0:T(8,128)S(1)}) custom-call(s32[1,1]{1,0:T(1,128)} %bitcast.4.counts_ref, f32[6,1024]{1,0:T(8,128)} %pv_ref.1, f32[6,1024]{1,0:T(8,128)} %aj_ref.1, f32[1,1024]{1,0:T(1,128)} %bitcast.5, f32[1,1024]{1,0:T(1,128)} %bitcast.6, s32[1,1024]{1,0:T(1,128)} %bitcast.7, ...), custom_call_target="tpu_custom_call" | custom-call | tf_op jit(solution)/shard_map/block_step/pallas_call | solution.py:278
  31.2 0.6 %copy.13 = f32[6,1024]{1,0:T(8,128)} copy(f32[6,1024]{1,0:T(8,128)S(1)} %get-tuple-element.3) | data formatting | bytes 49152
  31.9 0.6 %copy.15 = f32[12,256]{1,0:T(8,128)} copy(f32[12,256]{1,0:T(8,128)S(1)} %get-tuple-element.5) | data formatting | bytes 24576
  32.5 0.6 %copy.14 = f32[6,1024]{1,0:T(8,128)} copy(f32[6,1024]{1,0:T(8,128)S(1)} %get-tuple-element.4) | data formatting | bytes 49152
